TPU v7x, 512 devices: a whole 4x4x16 slice. The times are simulated.
512 devices in a mesh: grp: 16 (over z), dev: 32 (over x, y, core).
Axes of the slice: x: 4, y: 4, z: 16, core: 2. Of those that a mesh axis runs over, the one named last changes fastest.
Arguments:
- signs: int32 [1048576], P(('grp', 'dev')), may hold values from -1 to 1, as said below
- panel: float32 [1048576, 128], P(('grp', 'dev')), may hold values from -8 to 8
- samples: int32 [4096], replicated, may hold values from 0 to 1048575
Outputs:
- sketch: float32 [4096, 128], P(('grp', 'dev'))
Inputs may be any that keep to these rules, and one draw needn't show every extreme that they name: `signs`: each entry is -1 or +1.
All inputs are finite; a program needn't handle non-finite values.
Results may differ from a plain program's by a relative error of at most 0.000086.
Values sent between devices are 32-bit elements; how exact they have to be, the bound alone decides.
No kernel may reach another device: no remote copies, remote signals or barrier semaphores. Data moves between devices by JAX's collectives and lax.ppermute only.
A program may use at most 64 MiB of HBM per device.

v0:
```python
import math

import jax
import jax.numpy as jnp
from jax import lax
from jax.sharding import PartitionSpec as P

HIGHEST = lax.Precision.HIGHEST


def from_partner(value, axis, stride):
    mask = 2**stride
    pairs = [(source, source ^ mask) for source in range(lax.axis_size(axis))]
    return lax.ppermute(value, axis, pairs)


def sign_table(order):
    left = lax.broadcasted_iota(jnp.int32, (order, order), 0)
    right = lax.broadcasted_iota(jnp.int32, (order, order), 1)
    common = left & right
    parity = jnp.zeros((order, order), jnp.int32)
    for level in range(max(order.bit_length() - 1, 0)):
        parity = parity + (common >> level & 1)
    parity = parity & 1
    return (1 - 2 * parity).astype(jnp.float32)


def mix_local(flipped):
    rows, width = flipped.shape
    inner = min(rows, 128)
    outer = rows // inner
    cube = flipped.reshape(outer, inner, width)
    cube = jnp.einsum("ab,bjc->ajc", sign_table(outer), cube, precision=HIGHEST)
    cube = jnp.einsum("ij,ajc->aic", sign_table(inner), cube, precision=HIGHEST)
    return cube.reshape(rows, width)


def mix_leading(block):
    return jnp.einsum("ab,bjc->ajc", sign_table(block.shape[0]), block, precision=HIGHEST)


def local(signs, panel, samples):
    rows, width = panel.shape
    n_dev = lax.axis_size("dev")
    n_grp = lax.axis_size("grp")
    group = lax.axis_index("grp")
    member = lax.axis_index("dev")
    piece = rows // n_dev
    scale = 1.0 / math.sqrt(rows * n_dev * n_grp)
    flipped = panel * signs.astype(jnp.float32)[:, None]
    cube = mix_local(flipped).reshape(n_dev, piece, width)
    cube = lax.all_to_all(
        mix_leading(lax.all_to_all(cube, "dev", split_axis=0, concat_axis=0, tiled=True)),
        "dev",
        split_axis=0,
        concat_axis=0,
        tiled=True,
    )
    flat = cube.reshape(rows, width)
    for level in range(n_grp.bit_length() - 1):
        partner = from_partner(flat, "grp", level)
        upper = group >> level & 1 == 1
        flat = jnp.where(upper, partner - flat, flat + partner)
    flat = flat * scale
    group_of = samples // (n_dev * rows)
    inside = samples % (n_dev * rows)
    owned = (group_of == group) & (inside // rows == member)
    position = inside % rows
    taken = jnp.take(flat, jnp.where(owned, position, 0), axis=0)
    return lax.psum_scatter(
        jnp.where(owned[:, None], taken, 0.0), ("grp", "dev"), scatter_dimension=0, tiled=True
    )


def solution(mesh):
    return jax.shard_map(
        local,
        mesh=mesh,
        in_specs=(P(("grp", "dev")), P(("grp", "dev"), None), P()),
        out_specs=P(("grp", "dev"), None),
        check_vma=False,
    )
```

profile of v0, /device:TPU:24, one launch (start us, length us, event | category | flops | bytes accessed | tf_op | source)
XLA Modules:
  0.0 856.2 jit_solution(17298456138910964023)
XLA Ops:
  6.5 0.0 all-reduce.3.cloned.1.call-start
  6.5 0.7 convert_element_type.14
  7.2 1.6 broadcast_multiply_fusion
  8.8 1.5 fusion.4
  10.3 1.4 fusion.2
  11.7 23.6 %all_to_all.10 = f32[32,64,128]{2,1,0:T(8,128)S(1)} all-to-all(f32[32,64,128]{2,1,0:T(8,128)S(1)} %bitcast.17), channel_id=1, replica_groups=mesh['grp'=16,'dev'=32] {'dev'}, dimensions={0} | all-to-all | bytes 2097152 | tf_op jit(solution)/shard_map/all_to_all | solution.py:53
  35.3 1.6 fusion
  36.9 0.6 copy.10
  37.5 20.6 %all_to_all.11 = f32[32,64,128]{2,1,0:T(8,128)S(1)} all-to-all(f32[32,64,128]{2,1,0:T(8,128)S(1)} %copy.10), channel_id=1, replica_groups=mesh['grp'=16,'dev'=32] {'dev'}, dimensions={0} | all-to-all | bytes 2097152 | tf_op jit(solution)/shard_map/all_to_all | solution.py:52
  58.1 2.6 collective-permute-start
  60.7 24.7 %collective-permute-done = f32[2048,128]{1,0:T(8,128)S(1)} collective-permute-done((f32[2048,128]{1,0:T(8,128)S(1)}, f32[2048,128]{1,0:T(8,128)S(1)}, u32[]{:S(2)}, u32[]{:S(2)}) %collective-permute-start) | collective-permute-done | bytes 1048608 | tf_op jit(solution)/shard_map/ppermute | solution.py:14
  85.4 0.1 add_select_fusion.2
  85.5 4.1 collective-permute-start.1
  89.7 45.6 %collective-permute-done.1 = f32[2048,128]{1,0:T(8,128)S(1)} collective-permute-done((f32[2048,128]{1,0:T(8,128)S(1)}, f32[2048,128]{1,0:T(8,128)S(1)}, u32[]{:S(2)}, u32[]{:S(2)}) %collective-permute-start.1) | collective-permute-done | bytes 1048608 | tf_op jit(solution)/shard_map/ppermute | solution.py:14
  135.3 0.1 add_select_fusion.1
  135.4 0.0 copy-start
  135.4 8.9 %collective-permute-start.2 = (f32[2048,128]{1,0:T(8,128)S(1)}, f32[2048,128]{1,0:T(8,128)S(1)}, u32[]{:S(2)}, u32[]{:S(2)}) collective-permute-start(f32[2048,128]{1,0:T(8,128)S(1)} %add_select_fusion.1), channel_id=1, source_target_pairs={{0,128},{32,160},{64,192},{96,224},{128,0},{160,32},{192,64},{224,... | collective-permute-start | bytes 3145736 | tf_op jit(solution)/shard_map/ppermute | solution.py:14
  144.4 111.5 %collective-permute-done.2 = f32[2048,128]{1,0:T(8,128)S(1)} collective-permute-done((f32[2048,128]{1,0:T(8,128)S(1)}, f32[2048,128]{1,0:T(8,128)S(1)}, u32[]{:S(2)}, u32[]{:S(2)}) %collective-permute-start.2) | collective-permute-done | bytes 1048608 | tf_op jit(solution)/shard_map/ppermute | solution.py:14
  255.8 0.1 add_select_fusion
  256.0 58.2 %collective-permute-start.3 = (f32[2048,128]{1,0:T(8,128)S(1)}, f32[2048,128]{1,0:T(8,128)S(1)}, u32[]{:S(2)}, u32[]{:S(2)}) collective-permute-start(f32[2048,128]{1,0:T(8,128)S(1)} %add_select_fusion), channel_id=1, source_target_pairs={{0,256},{32,288},{64,320},{96,352},{128,384},{160,416},{192,448},{... | collective-permute-start | bytes 3145736 | tf_op jit(solution)/shard_map/ppermute | solution.py:14
  314.2 0.0 copy-done
  314.3 45.8 %collective-permute-done.3 = f32[2048,128]{1,0:T(8,128)S(1)} collective-permute-done((f32[2048,128]{1,0:T(8,128)S(1)}, f32[2048,128]{1,0:T(8,128)S(1)}, u32[]{:S(2)}, u32[]{:S(2)}) %collective-permute-start.3) | collective-permute-done | bytes 1048608 | tf_op jit(solution)/shard_map/ppermute | solution.py:14
  360.1 0.1 select_multiply_fusion
  360.2 10.8 %gather_fusion = f32[4096,128]{1,0:T(8,128)S(1)} fusion(f32[2048,128]{1,0:T(8,128)S(1)} %select_multiply_fusion, s32[4096]{0:T(1024)S(1)} %broadcast_clamp_fusion), kind=kCustom, calls=%fused_computation | custom fusion | bytes 4210688 | tf_op jit(solution)/shard_map/jit(_take)/gather | solution.py:69
  371.0 2.6 select_select_fusion
  373.7 0.0 all-reduce.3.cloned.1.call-update
  373.7 474.4 %all-reduce.3.cloned.1.call-done = f32[4096,128]{1,0:T(8,128)} async-done(((f32[4096,128]{1,0:T(8,128)}), f32[4096,128]{1,0:T(8,128)}) %all-reduce.3.cloned.1.call-update) | async-done | bytes 2097168
  848.1 1.3 constant_dynamic-slice_fusion
  (2 shorter events, 0.1 us)
Async XLA Ops:
  6.5 841.6 %all-reduce.3.cloned.1.call-start = ((), (), s32[]{:S(2)}) async-start(), calls=%async_computation.2 | async-start | bytes 4194304
  58.1 27.3 %collective-permute-start = (f32[2048,128]{1,0:T(8,128)S(1)}, f32[2048,128]{1,0:T(8,128)S(1)}, u32[]{:S(2)}, u32[]{:S(2)}) collective-permute-start(f32[2048,128]{1,0:T(8,128)S(1)} %bitcast.15), channel_id=1, source_target_pairs={{0,32},{32,0},{64,96},{96,64},{128,160},{160,128},{192,224},{224,1... | collective-permute-start | bytes 3145736 | tf_op jit(solution)/shard_map/ppermute | solution.py:14
  85.5 49.8 %collective-permute-start.1 = (f32[2048,128]{1,0:T(8,128)S(1)}, f32[2048,128]{1,0:T(8,128)S(1)}, u32[]{:S(2)}, u32[]{:S(2)}) collective-permute-start(f32[2048,128]{1,0:T(8,128)S(1)} %add_select_fusion.2), channel_id=1, source_target_pairs={{0,64},{32,96},{64,0},{96,32},{128,192},{160,224},{192,128},{224,1... | collective-permute-start | bytes 3145736 | tf_op jit(solution)/shard_map/ppermute | solution.py:14
  135.4 178.8 %copy-start = (s32[4096]{0:T(1024)S(1)}, s32[4096]{0:T(1024)}, u32[]{:S(2)}) copy-start(s32[4096]{0:T(1024)} %param.5) | copy-start | bytes 49156
  135.4 120.4 %collective-permute-start.2 = (f32[2048,128]{1,0:T(8,128)S(1)}, f32[2048,128]{1,0:T(8,128)S(1)}, u32[]{:S(2)}, u32[]{:S(2)}) collective-permute-start(f32[2048,128]{1,0:T(8,128)S(1)} %add_select_fusion.1), channel_id=1, source_target_pairs={{0,128},{32,160},{64,192},{96,224},{128,0},{160,32},{192,64},{224,... | collective-permute-start | bytes 3145736 | tf_op jit(solution)/shard_map/ppermute | solution.py:14
  256.0 104.1 %collective-permute-start.3 = (f32[2048,128]{1,0:T(8,128)S(1)}, f32[2048,128]{1,0:T(8,128)S(1)}, u32[]{:S(2)}, u32[]{:S(2)}) collective-permute-start(f32[2048,128]{1,0:T(8,128)S(1)} %add_select_fusion), channel_id=1, source_target_pairs={{0,256},{32,288},{64,320},{96,352},{128,384},{160,416},{192,448},{... | collective-permute-start | bytes 3145736 | tf_op jit(solution)/shard_map/ppermute | solution.py:14
Sparse Core Ops, SparseCore 0:
  373.8 474.2 all-reduce.2
where the time goes:
time: 858 us; the launch traced here: 856 us
  waiting for transfers between devices  702 us (82%)
  starting transfers between devices  73.9 us (9%)
  blocking collectives  44.2 us (5%)
  between operations  13.5 us (2%)
  local copies, waits for them, and re-layouts  12.7 us (1%)
    unnamed x2, waiting for transfers between devices  474 us
    ppermute x4, waiting for transfers between devices, from_partner(): return lax.ppermute(value, axis, pairs)  228 us
    ppermute x4, starting transfers between devices, from_partner(): return lax.ppermute(value, axis, pairs)  73.9 us
    all_to_all x1, blocking collectives, local(): lax.all_to_all(cube, 'dev', split_axis=0, concat_axis=0, tiled=True)  23.6 us
    all_to_all x1, blocking collectives, local(): lax.all_to_all(mix_leading(lax.all_to_all(cube, 'dev', split_axis=0, conc...  20.6 us
  transfers between devices with their start and end apart: 5, of which 5 were waited for; matrix products, arithmetic and copies ran while one was open for 0% of the time, Pallas kernels for 0%

commit v1 on v0

v1 whole, which is shorter than its diff:
```python
import functools
import math

import jax
import jax.numpy as jnp
from jax import lax
from jax.experimental import pallas as pl
from jax.experimental.pallas import tpu as pltpu
from jax.sharding import PartitionSpec as P

LANES = 128
SUB = 8


def odd_parity(value, bits):
    shift = 1
    while shift < bits:
        shift *= 2
    while shift > 1:
        shift //= 2
        value = value ^ (value >> shift)
    return value & 1


def columns_of(row):
    return jnp.broadcast_to(row, (LANES, LANES)).T


def partial_kernel(where_ref, samples_ref, signs_ref, panel_ref, out_ref, split_ref, *, tile):
    me, core = where_ref[0], where_ref[1]
    rows = panel_ref.shape[0]
    blocks = rows // LANES
    low = rows.bit_length() - 1
    lane_bits = LANES.bit_length() - 1

    for block in range(blocks):
        span = pl.ds(block * LANES, LANES)
        flipped = panel_ref[span, :] * columns_of(signs_ref[block : block + 1, :].astype(jnp.float32))
        high = flipped.astype(jnp.bfloat16)
        split_ref[span, :LANES] = high
        split_ref[span, LANES:] = (flipped - high.astype(jnp.float32)).astype(jnp.bfloat16)

    picks = samples_ref[...]
    device_odd = odd_parity((picks >> low) & me, 16)
    picks = (picks & (LANES - 1)) | (device_odd << lane_bits) | (((picks & (rows - 1)) >> lane_bits) << (lane_bits + 1))
    lane = lax.broadcasted_iota(jnp.int32, (tile * LANES // 2, LANES), 1) | LANES
    weights = split_ref[...]
    one, minus = jnp.float32(1), jnp.float32(-1)
    per_group = out_ref.shape[0] * SUB * 2 // LANES

    for start in range(0, picks.shape[0], tile):
        parts = []
        for line in range(start, start + tile):
            pairs = columns_of(picks[line : line + 1, :]).reshape(LANES // (2 * SUB), 2, SUB, LANES)
            parts.append(jnp.where(core == 0, pairs[:, 0], pairs[:, 1]).reshape(LANES // 2, LANES))
        own = jnp.concatenate(parts, axis=0)
        table = [jnp.where(odd_parity(own & lane, lane_bits + 1) == 0, one, minus).astype(jnp.bfloat16)]
        for level in range(blocks.bit_length() - 1):
            turn = jnp.where(own & (2 * LANES << level) == 0, one, minus).astype(jnp.bfloat16)
            table = table + [entry * turn for entry in table]
        left = jnp.concatenate(table, axis=1)
        both = jnp.dot(left, weights, preferred_element_type=jnp.float32)
        total = both[:, :LANES] + both[:, LANES:]
        groups = tile // per_group
        total = total.reshape(groups, out_ref.shape[0], SUB, LANES)
        for group in range(groups):
            out_ref[:, start // per_group + group] = total[group]


def partial_rows(where, samples, signs, panel, n_chip, n_grp):
    rows = panel.shape[0]
    vmem = pl.BlockSpec(memory_space=pltpu.VMEM)
    return pl.pallas_call(
        functools.partial(partial_kernel, tile=8),
        out_shape=jax.ShapeDtypeStruct((n_chip, n_grp, SUB, LANES), jnp.float32),
        in_specs=[pl.BlockSpec(memory_space=pltpu.SMEM), vmem, vmem, vmem],
        out_specs=vmem,
        scratch_shapes=[pltpu.VMEM((rows, 2 * LANES), jnp.bfloat16)],
        cost_estimate=pl.CostEstimate(flops=2 * 2048 * 2048 * 256, bytes_accessed=3 << 20, transcendentals=0),
    )(where, samples, signs, panel)


def local(signs, panel, samples):
    rows, width = panel.shape
    n_dev = lax.axis_size("dev")
    n_grp = lax.axis_size("grp")
    n_chip = n_dev // 2
    member = lax.axis_index("dev")
    core = member & 1
    me = lax.axis_index("grp") * n_dev + member
    scale = 1.0 / math.sqrt(rows * n_dev * n_grp)
    samples = samples.reshape(-1, LANES)
    signs = signs.reshape(-1, LANES)

    def part(side):
        return partial_rows(jnp.stack([me, side]), samples, signs, panel, n_chip, n_grp)

    swap = [(source, source ^ 1) for source in range(n_dev)]
    theirs = lax.ppermute(part(1 - core), "dev", swap)
    chip = part(core) + theirs
    cores = [[chip_at * 2 + side for chip_at in range(n_chip)] for side in range(2)]
    plane = lax.all_to_all(
        chip.reshape(n_chip, n_grp * SUB, width), "dev", 0, 0, axis_index_groups=cores, tiled=True
    ).sum(axis=0)
    column = lax.all_to_all(plane.reshape(n_grp, SUB, width), "grp", 0, 0, tiled=True)
    return column.sum(axis=0) * scale


def solution(mesh):
    return jax.shard_map(
        local,
        mesh=mesh,
        in_specs=(P(("grp", "dev")), P(("grp", "dev"), None), P()),
        out_specs=P(("grp", "dev"), None),
        check_vma=False,
    )
```

time: 858 us -> 67.4 us (0.08)
  the two profiles are of different devices: /device:TPU:24 before, /device:TPU:8 now
where the time goes in v1:
time: 67.4 us; the launch traced here: 67.1 us
  blocking collectives  51.5 us (76%)
  Pallas kernels  10.5 us (16%)
  other arithmetic  3.19 us (5%)
  starting transfers between devices  1.91 us (3%)
    all_to_all x1, blocking collectives, local(): lax.all_to_all(plane.reshape(n_grp, SUB, width), 'grp', 0, 0, tiled=True)  26.5 us
    all_to_all x1, blocking collectives, local(): lax.all_to_all(chip.reshape(n_chip, n_grp * SUB, width), 'dev', 0, 0, axi...  25 us
    pallas_call x2, Pallas kernels, partial_rows(): pl.pallas_call(functools.partial(partial_kernel, tile=8), out_shape=jax.S...  10.5 us
    ppermute x1, starting transfers between devices, local(): theirs = lax.ppermute(part(1 - core), 'dev', swap)  1.91 us
  transfers between devices with their start and end apart: 1, of which 0 were waited for; matrix products, arithmetic and copies ran while one was open for 1% of the time, Pallas kernels for 8%

profile of v1, /device:TPU:8, one launch (start us, length us, event | category | flops | bytes accessed | tf_op | source)
XLA Modules:
  0.0 67.1 jit_solution(2418654272959099169)
XLA Ops:
  0.0 0.6 pad_add_fusion.1.where_ref
  0.6 5.2 %shard_map.38 = f32[16,16,8,128]{3,2,1,0:T(8,128)} custom-call(s32[2]{0:T(128)} %pad_add_fusion.1.where_ref, s32[32,128]{1,0:T(8,128)} %bitcast.9, s32[16,128]{1,0:T(8,128)} %bitcast.11, f32[2048,128]{1,0:T(8,128)} %panel_ref.3), custom_call_target="tpu_custom_call" | custom-call | flops 2147483648 | bytes 3145728 | tf_op jit(solution)/shard_map/pallas_call | solution.py:73
  5.8 1.9 %collective-permute-start = (f32[16,16,8,128]{3,2,1,0:T(8,128)}, f32[16,16,8,128]{3,2,1,0:T(8,128)S(1)}, u32[]{:S(2)}, u32[]{:S(2)}) collective-permute-start(f32[16,16,8,128]{3,2,1,0:T(8,128)} %shard_map.38), channel_id=1, source_target_pairs={{0,1},{1,0},{2,3},{3,2},{4,5},{5,4},{6,7},{7,6},{8,9},{9,8},{10,11... | collective-permute-start | bytes 3145736 | tf_op jit(solution)/shard_map/ppermute | solution.py:99
  7.7 0.6 pad_add_fusion.where_ref
  8.3 5.3 %shard_map.37 = f32[16,16,8,128]{3,2,1,0:T(8,128)} custom-call(s32[2]{0:T(128)} %pad_add_fusion.where_ref, s32[32,128]{1,0:T(8,128)} %bitcast.10, s32[16,128]{1,0:T(8,128)} %bitcast.12, f32[2048,128]{1,0:T(8,128)} %panel_ref.3), custom_call_target="tpu_custom_call" | custom-call | flops 2147483648 | bytes 3145728 | tf_op jit(solution)/shard_map/pallas_call | solution.py:73
  13.6 0.0 collective-permute-done
  13.6 1.3 %add_bitcast_fusion = f32[16,128,128]{2,1,0:T(8,128)S(1)} fusion(f32[16,16,8,128]{3,2,1,0:T(8,128)} %shard_map.37, f32[16,16,8,128]{3,2,1,0:T(8,128)S(1)} %collective-permute-done), kind=kLoop, calls=%fused_computation | loop fusion | flops 262144 | bytes 3145728 | tf_op jit(solution)/shard_map/reshape | solution.py:103
  14.9 25.0 %all_to_all.10 = f32[16,128,128]{2,1,0:T(8,128)S(1)} all-to-all(f32[16,128,128]{2,1,0:T(8,128)S(1)} %add_bitcast_fusion), channel_id=1, replica_groups={{0,2,4,6,8,10,12,14,16,18,20,22,24,26,28,30},{1,3,5,7,9,11,13,15,17,19,..., dimensions={0} | all-to-all | bytes 2097152 | tf_op jit(solution)/shard_map/all_to_all | solution.py:102
  40.0 0.1 reduce_sum.18
  40.0 26.5 %all_to_all.11 = f32[16,8,128]{2,1,0:T(8,128)S(1)} all-to-all(f32[16,8,128]{2,1,0:T(8,128)S(1)} %bitcast.8), channel_id=1, replica_groups=mesh['grp'=16,'dev'=32] {'grp'}, dimensions={0} | all-to-all | bytes 131072 | tf_op jit(solution)/shard_map/all_to_all | solution.py:105
  66.5 0.6 broadcast_multiply_fusion
  (1 shorter events, 0.0 us)
Async XLA Ops:
  5.8 7.8 %collective-permute-start = (f32[16,16,8,128]{3,2,1,0:T(8,128)}, f32[16,16,8,128]{3,2,1,0:T(8,128)S(1)}, u32[]{:S(2)}, u32[]{:S(2)}) collective-permute-start(f32[16,16,8,128]{3,2,1,0:T(8,128)} %shard_map.38), channel_id=1, source_target_pairs={{0,1},{1,0},{2,3},{3,2},{4,5},{5,4},{6,7},{7,6},{8,9},{9,8},{10,11... | collective-permute-start | bytes 3145736 | tf_op jit(solution)/shard_map/ppermute | solution.py:99

commit v2 on v1

v2 whole, which is shorter than its diff:
```python
import functools
import math

import jax
import jax.numpy as jnp
from jax import lax
from jax.experimental import pallas as pl
from jax.experimental.pallas import tpu as pltpu
from jax.sharding import PartitionSpec as P

LANES = 128
SUB = 8
LANE_BITS = LANES.bit_length() - 1
TILE = 8
CHUNKS = 4


def odd_parity(value, bits):
    shift = 1
    while shift < bits:
        shift *= 2
    while shift > 1:
        shift //= 2
        value = value ^ (value >> shift)
    return value & 1


def columns_of(row):
    return jnp.broadcast_to(row, (LANES, LANES)).T


def coded(samples, rows, me):
    low = rows.bit_length() - 1
    device_odd = odd_parity((samples >> low) & me, 16)
    return (samples & (LANES - 1)) | (device_odd << LANE_BITS) | ((samples & (rows - LANES)) << 1)


def sign_rows(codes, start, blocks, side):
    parts = []
    for line in range(start, start + TILE):
        pairs = columns_of(codes[line : line + 1, :]).reshape(LANES // (2 * SUB), 2, SUB, LANES)
        parts.append(jnp.where(side == 0, pairs[:, 0], pairs[:, 1]).reshape(LANES // 2, LANES))
    own = jnp.concatenate(parts, axis=0)
    lane = lax.broadcasted_iota(jnp.int32, own.shape, 1) | LANES
    one, minus = jnp.float32(1), jnp.float32(-1)
    table = [jnp.where(odd_parity(own & lane, LANE_BITS + 1) == 0, one, minus).astype(jnp.bfloat16)]
    for level in range(blocks.bit_length() - 1):
        turn = jnp.where(own & (2 * LANES << level) == 0, one, minus).astype(jnp.bfloat16)
        table = table + [entry * turn for entry in table]
    return table


def sum_samples(codes, side, split_ref, out_ref, table=None):
    lines = codes.shape[0]
    blocks = split_ref.shape[0] // LANES
    chips = out_ref.shape[0]
    per_group = chips * SUB * 2 // LANES
    groups = TILE // per_group
    weights = split_ref[...]
    for start in range(0, lines, TILE):
        if start or table is None:
            table = sign_rows(codes, start, blocks, side)
        both = jnp.dot(jnp.concatenate(table, axis=1), weights, preferred_element_type=jnp.float32)
        total = (both[:, :LANES] + both[:, LANES:]).reshape(groups, chips, SUB, LANES)
        for group in range(groups):
            out_ref[:, start // per_group + group] = total[group]


def position():
    member = lax.axis_index("dev")
    return lax.axis_index("grp") * lax.axis_size("dev") + member, member & 1


def first_kernel(samples_ref, signs_ref, panel_ref, out_ref, split_ref, codes_ref, picks_ref, flips_ref, rows_ref, sems):
    me, core = position()
    rows = rows_ref.shape[0]
    blocks = rows // LANES
    part = rows // CHUNKS
    small = [
        pltpu.make_async_copy(samples_ref, picks_ref, sems.at[CHUNKS]),
        pltpu.make_async_copy(signs_ref, flips_ref, sems.at[CHUNKS + 1]),
    ]
    copies = []
    for chunk in range(CHUNKS):
        span = pl.ds(chunk * part, part)
        copies.append(pltpu.make_async_copy(panel_ref.at[span], rows_ref.at[span], sems.at[chunk]))
    for copy in small + copies:
        copy.start()
    small[0].wait()
    codes = coded(picks_ref[...], rows, me)
    codes_ref[...] = codes
    table = sign_rows(codes, 0, blocks, 1 - core)
    small[1].wait()
    for block in range(blocks):
        if block % (blocks // CHUNKS) == 0:
            copies[block // (blocks // CHUNKS)].wait()
        span = pl.ds(block * LANES, LANES)
        flipped = rows_ref[span, :] * columns_of(flips_ref[block : block + 1, :].astype(jnp.float32))
        high = flipped.astype(jnp.bfloat16)
        split_ref[span, :LANES] = high
        split_ref[span, LANES:] = (flipped - high.astype(jnp.float32)).astype(jnp.bfloat16)
    sum_samples(codes, 1 - core, split_ref, out_ref, table)


def second_kernel(codes_ref, split_ref, out_ref):
    core = lax.axis_index("dev") & 1
    sum_samples(codes_ref[...], core, split_ref, out_ref)


def local(signs, panel, samples):
    rows, width = panel.shape
    n_dev = lax.axis_size("dev")
    n_grp = lax.axis_size("grp")
    n_chip = n_dev // 2
    scale = 1.0 / math.sqrt(rows * n_dev * n_grp)
    samples = samples.reshape(-1, LANES)
    signs = signs.reshape(-1, LANES)
    vmem = pl.BlockSpec(memory_space=pltpu.VMEM)
    hbm = pl.BlockSpec(memory_space=pltpu.HBM)
    partial = pltpu.VMEM((n_chip, n_grp, SUB, LANES), jnp.float32)
    params = pltpu.CompilerParams(vmem_limit_bytes=16 << 20)
    cost = pl.CostEstimate(flops=2 * 2048 * 2048 * 256, bytes_accessed=3 << 20, transcendentals=0)

    theirs, split, codes = pl.pallas_call(
        first_kernel,
        out_shape=(partial, pltpu.VMEM((rows, 2 * LANES), jnp.bfloat16), pltpu.VMEM(samples.shape, jnp.int32)),
        in_specs=[hbm, hbm, hbm],
        out_specs=(vmem, vmem, vmem),
        scratch_shapes=[
            pltpu.VMEM(samples.shape, jnp.int32),
            pltpu.VMEM(signs.shape, jnp.int32),
            pltpu.VMEM((rows, LANES), jnp.float32),
            pltpu.SemaphoreType.DMA((CHUNKS + 2,)),
        ],
        compiler_params=params,
        cost_estimate=cost,
    )(*(pltpu.with_memory_space_constraint(value, pltpu.HBM) for value in (samples, signs, panel)))
    theirs = lax.ppermute(theirs, "dev", [(source, source ^ 1) for source in range(n_dev)])
    ours = pl.pallas_call(
        second_kernel,
        out_shape=partial,
        in_specs=[vmem, vmem],
        out_specs=vmem,
        compiler_params=params,
        cost_estimate=cost,
    )(codes, split)
    chip = ours + theirs
    cores = [[chip_at * 2 + side for chip_at in range(n_chip)] for side in range(2)]
    plane = lax.all_to_all(
        chip.reshape(n_chip, n_grp * SUB, width), "dev", 0, 0, axis_index_groups=cores, tiled=True
    ).sum(axis=0)
    column = lax.all_to_all(plane.reshape(n_grp, SUB, width), "grp", 0, 0, tiled=True)
    return column.sum(axis=0) * scale


def solution(mesh):
    return jax.shard_map(
        local,
        mesh=mesh,
        in_specs=(P(("grp", "dev")), P(("grp", "dev"), None), P()),
        out_specs=P(("grp", "dev"), None),
        check_vma=False,
    )
```

time: 67.4 us -> 61.3 us (0.909)
  Pallas kernels: 10.5 us -> 6.8 us
  other arithmetic: 3.19 us -> 0.8 us
    pallas_call x2, Pallas kernels: 10.5 us -> 6.8 us  [the longest x1 4.08 us: local(): pl.pallas_call(first_kernel, out_shape=(partial, pltpu.VMEM((rows, 2 * LA...]
    reshape x1, other arithmetic: 1.34 us -> 0.13 us  [local(): chip.reshape(n_chip, n_grp * SUB, width)]
    another operation x2 -> x0, other arithmetic: 1.18 us -> none  [part(): jnp.stack([me, side])]
  transfers between devices with their start and end apart: 1 -> 1, of which waited for: 0 -> 0; matrix products, arithmetic and copies ran while one was open for 1% -> 0% of each run, Pallas kernels for 8% -> 4%
where the time goes in v2:
time: 61.3 us; the launch traced here: 61 us
  blocking collectives  51.5 us (84%)
  Pallas kernels  6.8 us (11%)
  starting transfers between devices  1.92 us (3%)
  other arithmetic  0.8 us (1%)
    all_to_all x1, blocking collectives, local(): lax.all_to_all(plane.reshape(n_grp, SUB, width), 'grp', 0, 0, tiled=True)  26.4 us
    all_to_all x1, blocking collectives, local(): lax.all_to_all(chip.reshape(n_chip, n_grp * SUB, width), 'dev', 0, 0, axi...  25 us
    pallas_call x1, Pallas kernels, local(): pl.pallas_call(first_kernel, out_shape=(partial, pltpu.VMEM((rows, 2 * LA...  4.08 us
    pallas_call x1, Pallas kernels, local(): pl.pallas_call(second_kernel, out_shape=partial, in_specs=[vmem, vmem], o...  2.72 us
    ppermute x1, starting transfers between devices, local(): lax.ppermute(theirs, 'dev', [(source, source ^ 1) for source in range(n_d...  1.92 us
  transfers between devices with their start and end apart: 1, of which 0 were waited for; matrix products, arithmetic and copies ran while one was open for 0% of the time, Pallas kernels for 4%

profile of v2, /device:TPU:8, one launch (start us, length us, event | category | flops | bytes accessed | tf_op | source)
XLA Modules:
  0.0 61.0 jit_solution(8139677227495114596)
XLA Ops:
  0.0 4.1 %shard_map.37 = (f32[16,16,8,128]{3,2,1,0:T(8,128)S(1)}, bf16[2048,256]{1,0:T(8,128)(2,1)S(1)}, s32[32,128]{1,0:T(8,128)S(1)}) custom-call(s32[32,128]{1,0:T(8,128)} %bitcast.6, s32[16,128]{1,0:T(8,128)} %bitcast.7, f32[2048,128]{1,0:T(8,128)} %panel_ref.1), custom_call_target="tpu_custom_call" | custom-call | flops 2147483648 | bytes 3145728 | tf_op jit(solution)/shard_map/pallas_call | solution.py:124
  4.1 1.9 %collective-permute-start = (f32[16,16,8,128]{3,2,1,0:T(8,128)S(1)}, f32[16,16,8,128]{3,2,1,0:T(8,128)S(1)}, u32[]{:S(2)}, u32[]{:S(2)}) collective-permute-start(f32[16,16,8,128]{3,2,1,0:T(8,128)S(1)} %get-tuple-element.10), channel_id=1, source_target_pairs={{0,1},{1,0},{2,3},{3,2},{4,5},{5,4},{6,7},{7,6},{8,9},{9,8},{10,11... | collective-permute-start | bytes 3145736 | tf_op jit(solution)/shard_map/ppermute | solution.py:138
  6.0 2.7 %shard_map.38 = f32[16,16,8,128]{3,2,1,0:T(8,128)S(1)} custom-call(s32[32,128]{1,0:T(8,128)S(1)} %get-tuple-element.8.codes_ref, bf16[2048,256]{1,0:T(8,128)(2,1)S(1)} %get-tuple-element.9.split_ref), custom_call_target="tpu_custom_call" | custom-call | flops 2147483648 | bytes 3145728 | tf_op jit(solution)/shard_map/pallas_call | solution.py:139
  8.7 0.0 collective-permute-done
  8.8 0.1 add_bitcast_fusion
  8.9 25.0 %all_to_all.10 = f32[16,128,128]{2,1,0:T(8,128)S(1)} all-to-all(f32[16,128,128]{2,1,0:T(8,128)S(1)} %add_bitcast_fusion), channel_id=1, replica_groups={{0,2,4,6,8,10,12,14,16,18,20,22,24,26,28,30},{1,3,5,7,9,11,13,15,17,19,..., dimensions={0} | all-to-all | bytes 2097152 | tf_op jit(solution)/shard_map/all_to_all | solution.py:149
  33.9 0.1 reduce_sum.18
  34.0 26.4 %all_to_all.11 = f32[16,8,128]{2,1,0:T(8,128)S(1)} all-to-all(f32[16,8,128]{2,1,0:T(8,128)S(1)} %bitcast.5), channel_id=1, replica_groups=mesh['grp'=16,'dev'=32] {'grp'}, dimensions={0} | all-to-all | bytes 131072 | tf_op jit(solution)/shard_map/all_to_all | solution.py:152
  60.4 0.6 broadcast_multiply_fusion
  (1 shorter events, 0.0 us)
Async XLA Ops:
  4.1 4.7 %collective-permute-start = (f32[16,16,8,128]{3,2,1,0:T(8,128)S(1)}, f32[16,16,8,128]{3,2,1,0:T(8,128)S(1)}, u32[]{:S(2)}, u32[]{:S(2)}) collective-permute-start(f32[16,16,8,128]{3,2,1,0:T(8,128)S(1)} %get-tuple-element.10), channel_id=1, source_target_pairs={{0,1},{1,0},{2,3},{3,2},{4,5},{5,4},{6,7},{7,6},{8,9},{9,8},{10,11... | collective-permute-start | bytes 3145736 | tf_op jit(solution)/shard_map/ppermute | solution.py:138

commit v3 on v2

--- a/solution.py
+++ b/solution.py
@@ -13,6 +13,8 @@
 LANE_BITS = LANES.bit_length() - 1
 TILE = 8
 CHUNKS = 4
+FIRST_GROUP = 8
+FIRST_CHIP = 15
 
 
 def odd_parity(value, bits):
@@ -63,7 +65,9 @@
         both = jnp.dot(jnp.concatenate(table, axis=1), weights, preferred_element_type=jnp.float32)
         total = (both[:, :LANES] + both[:, LANES:]).reshape(groups, chips, SUB, LANES)
         for group in range(groups):
-            out_ref[:, start // per_group + group] = total[group]
+            place = (start // per_group + group - FIRST_GROUP) % out_ref.shape[1]
+            for chip in range(chips):
+                out_ref[(chip - FIRST_CHIP) % chips, place] = total[group, chip]
 
 
 def position():
@@ -145,11 +149,23 @@
         cost_estimate=cost,
     )(codes, split)
     chip = ours + theirs
-    cores = [[chip_at * 2 + side for chip_at in range(n_chip)] for side in range(2)]
+    chips = [(chip_at + FIRST_CHIP) % n_chip for chip_at in range(n_chip)]
     plane = lax.all_to_all(
-        chip.reshape(n_chip, n_grp * SUB, width), "dev", 0, 0, axis_index_groups=cores, tiled=True
+        chip.reshape(n_chip, n_grp * SUB, width),
+        "dev",
+        0,
+        0,
+        axis_index_groups=[[chip_at * 2 + side for chip_at in chips] for side in range(2)],
+        tiled=True,
     ).sum(axis=0)
-    column = lax.all_to_all(plane.reshape(n_grp, SUB, width), "grp", 0, 0, tiled=True)
+    column = lax.all_to_all(
+        plane.reshape(n_grp, SUB, width),
+        "grp",
+        0,
+        0,
+        axis_index_groups=[[(group + FIRST_GROUP) % n_grp for group in range(n_grp)]],
+        tiled=True,
+    )
     return column.sum(axis=0) * scale
 
 

time: 61.3 us -> 54.3 us (0.89)
  the two profiles are of different devices: /device:TPU:8 before, /device:TPU:24 now
where the time goes in v3:
time: 54.3 us; the launch traced here: 53.6 us
  blocking collectives  44.1 us (81%)
  Pallas kernels  6.8 us (13%)
  starting transfers between devices  1.92 us (4%)
  other arithmetic  0.8 us (1%)
    all_to_all x1, blocking collectives, local(): lax.all_to_all(chip.reshape(n_chip, n_grp * SUB, width), 'dev', 0, 0, axi...  25.1 us
    all_to_all x1, blocking collectives, local(): lax.all_to_all(plane.reshape(n_grp, SUB, width), 'grp', 0, 0, axis_index_...  19 us
    pallas_call x1, Pallas kernels, local(): pl.pallas_call(first_kernel, out_shape=(partial, pltpu.VMEM((rows, 2 * LA...  4.08 us
    pallas_call x1, Pallas kernels, local(): pl.pallas_call(second_kernel, out_shape=partial, in_specs=[vmem, vmem], o...  2.72 us
    ppermute x1, starting transfers between devices, local(): lax.ppermute(theirs, 'dev', [(source, source ^ 1) for source in range(n_d...  1.92 us
  transfers between devices with their start and end apart: 1, of which 0 were waited for; matrix products, arithmetic and copies ran while one was open for 0% of the time, Pallas kernels for 5%

profile of v3, /device:TPU:24, one launch (start us, length us, event | category | flops | bytes accessed | tf_op | source)
XLA Modules:
  0.0 53.6 jit_solution(16493556318411187658)
XLA Ops:
  0.0 4.1 %shard_map.37 = (f32[16,16,8,128]{3,2,1,0:T(8,128)S(1)}, bf16[2048,256]{1,0:T(8,128)(2,1)S(1)}, s32[32,128]{1,0:T(8,128)S(1)}) custom-call(s32[32,128]{1,0:T(8,128)} %bitcast.6, s32[16,128]{1,0:T(8,128)} %bitcast.7, f32[2048,128]{1,0:T(8,128)} %panel_ref.1), custom_call_target="tpu_custom_call" | custom-call | flops 2147483648 | bytes 3145728 | tf_op jit(solution)/shard_map/pallas_call | solution.py:128
  4.1 1.9 %collective-permute-start = (f32[16,16,8,128]{3,2,1,0:T(8,128)S(1)}, f32[16,16,8,128]{3,2,1,0:T(8,128)S(1)}, u32[]{:S(2)}, u32[]{:S(2)}) collective-permute-start(f32[16,16,8,128]{3,2,1,0:T(8,128)S(1)} %get-tuple-element.10), channel_id=1, source_target_pairs={{0,1},{1,0},{2,3},{3,2},{4,5},{5,4},{6,7},{7,6},{8,9},{9,8},{10,11... | collective-permute-start | bytes 3145736 | tf_op jit(solution)/shard_map/ppermute | solution.py:142
  6.0 2.7 %shard_map.38 = f32[16,16,8,128]{3,2,1,0:T(8,128)S(1)} custom-call(s32[32,128]{1,0:T(8,128)S(1)} %get-tuple-element.8.codes_ref, bf16[2048,256]{1,0:T(8,128)(2,1)S(1)} %get-tuple-element.9.split_ref), custom_call_target="tpu_custom_call" | custom-call | flops 2147483648 | bytes 3145728 | tf_op jit(solution)/shard_map/pallas_call | solution.py:143
  8.7 0.0 collective-permute-done
  8.8 0.1 add_bitcast_fusion
  8.9 25.1 %all_to_all.10 = f32[16,128,128]{2,1,0:T(8,128)S(1)} all-to-all(f32[16,128,128]{2,1,0:T(8,128)S(1)} %add_bitcast_fusion), channel_id=1, replica_groups={{30,0,2,4,6,8,10,12,14,16,18,20,22,24,26,28},{31,1,3,5,7,9,11,13,15,17,..., dimensions={0} | all-to-all | bytes 2097152 | tf_op jit(solution)/shard_map/all_to_all | solution.py:153
  34.0 0.1 reduce_sum.18
  34.1 19.0 %all_to_all.11 = f32[16,8,128]{2,1,0:T(8,128)S(1)} all-to-all(f32[16,8,128]{2,1,0:T(8,128)S(1)} %bitcast.5), channel_id=1, replica_groups={{256,288,320,352,384,416,448,480,0,32,64,96,128,160,192,224},{257,289,3..., dimensions={0} | all-to-all | bytes 131072 | tf_op jit(solution)/shard_map/all_to_all | solution.py:161
  53.0 0.6 %broadcast_multiply_fusion = f32[8,128]{1,0:T(8,128)} fusion(f32[8,128]{1,0:T(8,128)S(1)} %reduce_sum.19), kind=kLoop, calls=%fused_computation.1 | loop fusion | flops 1024 | bytes 8192 | tf_op jit(solution)/shard_map/mul | solution.py:169
  (1 shorter events, 0.0 us)
Async XLA Ops:
  4.1 4.7 %collective-permute-start = (f32[16,16,8,128]{3,2,1,0:T(8,128)S(1)}, f32[16,16,8,128]{3,2,1,0:T(8,128)S(1)}, u32[]{:S(2)}, u32[]{:S(2)}) collective-permute-start(f32[16,16,8,128]{3,2,1,0:T(8,128)S(1)} %get-tuple-element.10), channel_id=1, source_target_pairs={{0,1},{1,0},{2,3},{3,2},{4,5},{5,4},{6,7},{7,6},{8,9},{9,8},{10,11... | collective-permute-start | bytes 3145736 | tf_op jit(solution)/shard_map/ppermute | solution.py:142

commit v4 on v3

--- a/solution.py
+++ b/solution.py
@@ -13,18 +13,12 @@
 LANE_BITS = LANES.bit_length() - 1
 TILE = 8
 CHUNKS = 4
-FIRST_GROUP = 8
-FIRST_CHIP = 15
+GROUPS = tuple((8 + at) % 16 for at in range(16))
+CHIPS = tuple((10 + at) % 16 for at in range(16))
 
 
-def odd_parity(value, bits):
-    shift = 1
-    while shift < bits:
-        shift *= 2
-    while shift > 1:
-        shift //= 2
-        value = value ^ (value >> shift)
-    return value & 1
+def odd_parity(value):
+    return lax.population_count(value) & 1
 
 
 def columns_of(row):
@@ -33,7 +27,7 @@
 
 def coded(samples, rows, me):
     low = rows.bit_length() - 1
-    device_odd = odd_parity((samples >> low) & me, 16)
+    device_odd = odd_parity((samples >> low) & me)
     return (samples & (LANES - 1)) | (device_odd << LANE_BITS) | ((samples & (rows - LANES)) << 1)
 
 
@@ -45,7 +39,7 @@
     own = jnp.concatenate(parts, axis=0)
     lane = lax.broadcasted_iota(jnp.int32, own.shape, 1) | LANES
     one, minus = jnp.float32(1), jnp.float32(-1)
-    table = [jnp.where(odd_parity(own & lane, LANE_BITS + 1) == 0, one, minus).astype(jnp.bfloat16)]
+    table = [jnp.where(odd_parity(own & lane) == 0, one, minus).astype(jnp.bfloat16)]
     for level in range(blocks.bit_length() - 1):
         turn = jnp.where(own & (2 * LANES << level) == 0, one, minus).astype(jnp.bfloat16)
         table = table + [entry * turn for entry in table]
@@ -65,9 +59,9 @@
         both = jnp.dot(jnp.concatenate(table, axis=1), weights, preferred_element_type=jnp.float32)
         total = (both[:, :LANES] + both[:, LANES:]).reshape(groups, chips, SUB, LANES)
         for group in range(groups):
-            place = (start // per_group + group - FIRST_GROUP) % out_ref.shape[1]
+            place = GROUPS.index(start // per_group + group)
             for chip in range(chips):
-                out_ref[(chip - FIRST_CHIP) % chips, place] = total[group, chip]
+                out_ref[CHIPS.index(chip), place] = total[group, chip]
 
 
 def position():
@@ -94,10 +88,9 @@
     codes = coded(picks_ref[...], rows, me)
     codes_ref[...] = codes
     table = sign_rows(codes, 0, blocks, 1 - core)
-    small[1].wait()
+    for copy in small[1:] + copies:
+        copy.wait()
     for block in range(blocks):
-        if block % (blocks // CHUNKS) == 0:
-            copies[block // (blocks // CHUNKS)].wait()
         span = pl.ds(block * LANES, LANES)
         flipped = rows_ref[span, :] * columns_of(flips_ref[block : block + 1, :].astype(jnp.float32))
         high = flipped.astype(jnp.bfloat16)
@@ -149,13 +142,12 @@
         cost_estimate=cost,
     )(codes, split)
     chip = ours + theirs
-    chips = [(chip_at + FIRST_CHIP) % n_chip for chip_at in range(n_chip)]
     plane = lax.all_to_all(
         chip.reshape(n_chip, n_grp * SUB, width),
         "dev",
         0,
         0,
-        axis_index_groups=[[chip_at * 2 + side for chip_at in chips] for side in range(2)],
+        axis_index_groups=[[chip_at * 2 + side for chip_at in CHIPS] for side in range(2)],
         tiled=True,
     ).sum(axis=0)
     column = lax.all_to_all(
@@ -163,7 +155,7 @@
         "grp",
         0,
         0,
-        axis_index_groups=[[(group + FIRST_GROUP) % n_grp for group in range(n_grp)]],
+        axis_index_groups=[GROUPS],
         tiled=True,
     )
     return column.sum(axis=0) * scale

time: 54.3 us -> 53.3 us (0.982)
  transfers between devices with their start and end apart: 1 -> 1, of which waited for: 0 -> 1; matrix products, arithmetic and copies ran while one was open for 0% -> 0% of each run, Pallas kernels for 5% -> 5%
where the time goes in v4:
time: 53.3 us; the launch traced here: 53 us
  blocking collectives  43.8 us (82%)
  Pallas kernels  6.42 us (12%)
  starting transfers between devices  1.92 us (4%)
  other arithmetic  0.8 us (2%)
    all_to_all x1, blocking collectives, local(): lax.all_to_all(chip.reshape(n_chip, n_grp * SUB, width), 'dev', 0, 0, axi...  25.1 us
    all_to_all x1, blocking collectives, local(): lax.all_to_all(plane.reshape(n_grp, SUB, width), 'grp', 0, 0, axis_index_...  18.6 us
    pallas_call x1, Pallas kernels, local(): pl.pallas_call(first_kernel, out_shape=(partial, pltpu.VMEM((rows, 2 * LA...  3.86 us
    pallas_call x1, Pallas kernels, local(): pl.pallas_call(second_kernel, out_shape=partial, in_specs=[vmem, vmem], o...  2.56 us
    ppermute x1, starting transfers between devices, local(): lax.ppermute(theirs, 'dev', [(source, source ^ 1) for source in range(n_d...  1.92 us
  transfers between devices with their start and end apart: 1, of which 1 were waited for; matrix products, arithmetic and copies ran while one was open for 0% of the time, Pallas kernels for 5%

profile of v4, /device:TPU:24, one launch (start us, length us, event | category | flops | bytes accessed | tf_op | source)
XLA Modules:
  0.0 53.0 jit_solution(8730850986907742462)
XLA Ops:
  0.0 3.9 %shard_map.37 = (f32[16,16,8,128]{3,2,1,0:T(8,128)S(1)}, bf16[2048,256]{1,0:T(8,128)(2,1)S(1)}, s32[32,128]{1,0:T(8,128)S(1)}) custom-call(s32[32,128]{1,0:T(8,128)} %bitcast.6, s32[16,128]{1,0:T(8,128)} %bitcast.7, f32[2048,128]{1,0:T(8,128)} %panel_ref.1), custom_call_target="tpu_custom_call" | custom-call | flops 2147483648 | bytes 3145728 | tf_op jit(solution)/shard_map/pallas_call | solution.py:121
  3.9 1.9 %collective-permute-start = (f32[16,16,8,128]{3,2,1,0:T(8,128)S(1)}, f32[16,16,8,128]{3,2,1,0:T(8,128)S(1)}, u32[]{:S(2)}, u32[]{:S(2)}) collective-permute-start(f32[16,16,8,128]{3,2,1,0:T(8,128)S(1)} %get-tuple-element.10), channel_id=1, source_target_pairs={{0,1},{1,0},{2,3},{3,2},{4,5},{5,4},{6,7},{7,6},{8,9},{9,8},{10,11... | collective-permute-start | bytes 3145736 | tf_op jit(solution)/shard_map/ppermute | solution.py:135
  5.8 2.6 %shard_map.38 = f32[16,16,8,128]{3,2,1,0:T(8,128)S(1)} custom-call(s32[32,128]{1,0:T(8,128)S(1)} %get-tuple-element.8.codes_ref, bf16[2048,256]{1,0:T(8,128)(2,1)S(1)} %get-tuple-element.9.split_ref), custom_call_target="tpu_custom_call" | custom-call | flops 2147483648 | bytes 3145728 | tf_op jit(solution)/shard_map/pallas_call | solution.py:136
  8.4 0.1 collective-permute-done
  8.4 0.1 add_bitcast_fusion
  8.6 25.1 %all_to_all.10 = f32[16,128,128]{2,1,0:T(8,128)S(1)} all-to-all(f32[16,128,128]{2,1,0:T(8,128)S(1)} %add_bitcast_fusion), channel_id=1, replica_groups={{20,22,24,26,28,30,0,2,4,6,8,10,12,14,16,18},{21,23,25,27,29,31,1,3,5,7..., dimensions={0} | all-to-all | bytes 2097152 | tf_op jit(solution)/shard_map/all_to_all | solution.py:145
  33.7 0.1 reduce_sum.18
  33.7 18.6 %all_to_all.11 = f32[16,8,128]{2,1,0:T(8,128)S(1)} all-to-all(f32[16,8,128]{2,1,0:T(8,128)S(1)} %bitcast.5), channel_id=1, replica_groups={{256,288,320,352,384,416,448,480,0,32,64,96,128,160,192,224},{257,289,3..., dimensions={0} | all-to-all | bytes 131072 | tf_op jit(solution)/shard_map/all_to_all | solution.py:153
  52.4 0.6 %broadcast_multiply_fusion = f32[8,128]{1,0:T(8,128)} fusion(f32[8,128]{1,0:T(8,128)S(1)} %reduce_sum.19), kind=kLoop, calls=%fused_computation.1 | loop fusion | flops 1024 | bytes 8192 | tf_op jit(solution)/shard_map/mul | solution.py:161
  (1 shorter events, 0.0 us)
Async XLA Ops:
  3.9 4.6 %collective-permute-start = (f32[16,16,8,128]{3,2,1,0:T(8,128)S(1)}, f32[16,16,8,128]{3,2,1,0:T(8,128)S(1)}, u32[]{:S(2)}, u32[]{:S(2)}) collective-permute-start(f32[16,16,8,128]{3,2,1,0:T(8,128)S(1)} %get-tuple-element.10), channel_id=1, source_target_pairs={{0,1},{1,0},{2,3},{3,2},{4,5},{5,4},{6,7},{7,6},{8,9},{9,8},{10,11... | collective-permute-start | bytes 3145736 | tf_op jit(solution)/shard_map/ppermute | solution.py:135

commit v5 on v4

--- a/solution.py
+++ b/solution.py
@@ -11,9 +11,9 @@
 LANES = 128
 SUB = 8
 LANE_BITS = LANES.bit_length() - 1
-TILE = 8
+TILE = 4
 CHUNKS = 4
-GROUPS = tuple((8 + at) % 16 for at in range(16))
+GROUPS = (9, 0, 15, 1, 14, 2, 13, 3, 12, 4, 11, 5, 10, 6, 8, 7)
 CHIPS = tuple((10 + at) % 16 for at in range(16))
 
 
@@ -82,7 +82,9 @@
     for chunk in range(CHUNKS):
         span = pl.ds(chunk * part, part)
         copies.append(pltpu.make_async_copy(panel_ref.at[span], rows_ref.at[span], sems.at[chunk]))
-    for copy in small + copies:
+    for chunk, copy in enumerate(copies):
+        copy.start(priority=chunk % 2)
+    for copy in small:
         copy.start()
     small[0].wait()
     codes = coded(picks_ref[...], rows, me)

time: 53.3 us -> 52.3 us (0.981)
  blocking collectives: 43.8 us -> 42.9 us
    all_to_all x1, blocking collectives: 18.6 us -> 17.9 us  [local(): lax.all_to_all(plane.reshape(n_grp, SUB, width), 'grp', 0, 0, axis_index_...]
where the time goes in v5:
time: 52.3 us; the launch traced here: 52.1 us
  blocking collectives  42.9 us (82%)
  Pallas kernels  6.29 us (12%)
  starting transfers between devices  1.92 us (4%)
  other arithmetic  0.8 us (2%)
    all_to_all x1, blocking collectives, local(): lax.all_to_all(chip.reshape(n_chip, n_grp * SUB, width), 'dev', 0, 0, axi...  25 us
    all_to_all x1, blocking collectives, local(): lax.all_to_all(plane.reshape(n_grp, SUB, width), 'grp', 0, 0, axis_index_...  17.9 us
    pallas_call x1, Pallas kernels, local(): pl.pallas_call(first_kernel, out_shape=(partial, pltpu.VMEM((rows, 2 * LA...  3.84 us
    pallas_call x1, Pallas kernels, local(): pl.pallas_call(second_kernel, out_shape=partial, in_specs=[vmem, vmem], o...  2.46 us
    ppermute x1, starting transfers between devices, local(): lax.ppermute(theirs, 'dev', [(source, source ^ 1) for source in range(n_d...  1.92 us
  transfers between devices with their start and end apart: 1, of which 1 were waited for; matrix products, arithmetic and copies ran while one was open for 0% of the time, Pallas kernels for 5%

profile of v5, /device:TPU:24, one launch (start us, length us, event | category | flops | bytes accessed | tf_op | source)
XLA Modules:
  0.0 52.1 jit_solution(3556663061695304027)
XLA Ops:
  0.0 3.8 %shard_map.37 = (f32[16,16,8,128]{3,2,1,0:T(8,128)S(1)}, bf16[2048,256]{1,0:T(8,128)(2,1)S(1)}, s32[32,128]{1,0:T(8,128)S(1)}) custom-call(s32[32,128]{1,0:T(8,128)} %bitcast.6, s32[16,128]{1,0:T(8,128)} %bitcast.7, f32[2048,128]{1,0:T(8,128)} %panel_ref.1), custom_call_target="tpu_custom_call" | custom-call | flops 2147483648 | bytes 3145728 | tf_op jit(solution)/shard_map/pallas_call | solution.py:123
  3.8 1.9 %collective-permute-start = (f32[16,16,8,128]{3,2,1,0:T(8,128)S(1)}, f32[16,16,8,128]{3,2,1,0:T(8,128)S(1)}, u32[]{:S(2)}, u32[]{:S(2)}) collective-permute-start(f32[16,16,8,128]{3,2,1,0:T(8,128)S(1)} %get-tuple-element.10), channel_id=1, source_target_pairs={{0,1},{1,0},{2,3},{3,2},{4,5},{5,4},{6,7},{7,6},{8,9},{9,8},{10,11... | collective-permute-start | bytes 3145736 | tf_op jit(solution)/shard_map/ppermute | solution.py:137
  5.8 2.5 %shard_map.38 = f32[16,16,8,128]{3,2,1,0:T(8,128)S(1)} custom-call(s32[32,128]{1,0:T(8,128)S(1)} %get-tuple-element.8.codes_ref, bf16[2048,256]{1,0:T(8,128)(2,1)S(1)} %get-tuple-element.9.split_ref), custom_call_target="tpu_custom_call" | custom-call | flops 2147483648 | bytes 3145728 | tf_op jit(solution)/shard_map/pallas_call | solution.py:138
  8.2 0.2 collective-permute-done
  8.4 0.1 add_bitcast_fusion
  8.5 25.0 %all_to_all.10 = f32[16,128,128]{2,1,0:T(8,128)S(1)} all-to-all(f32[16,128,128]{2,1,0:T(8,128)S(1)} %add_bitcast_fusion), channel_id=1, replica_groups={{20,22,24,26,28,30,0,2,4,6,8,10,12,14,16,18},{21,23,25,27,29,31,1,3,5,7..., dimensions={0} | all-to-all | bytes 2097152 | tf_op jit(solution)/shard_map/all_to_all | solution.py:147
  33.5 0.1 reduce_sum.18
  33.6 17.9 %all_to_all.11 = f32[16,8,128]{2,1,0:T(8,128)S(1)} all-to-all(f32[16,8,128]{2,1,0:T(8,128)S(1)} %bitcast.5), channel_id=1, replica_groups={{288,0,480,32,448,64,416,96,384,128,352,160,320,192,256,224},{289,1,481..., dimensions={0} | all-to-all | bytes 131072 | tf_op jit(solution)/shard_map/all_to_all | solution.py:155
  51.5 0.6 %broadcast_multiply_fusion = f32[8,128]{1,0:T(8,128)} fusion(f32[8,128]{1,0:T(8,128)S(1)} %reduce_sum.19), kind=kLoop, calls=%fused_computation.1 | loop fusion | flops 1024 | bytes 8192 | tf_op jit(solution)/shard_map/mul | solution.py:163
  (1 shorter events, 0.0 us)
Async XLA Ops:
  3.8 4.6 %collective-permute-start = (f32[16,16,8,128]{3,2,1,0:T(8,128)S(1)}, f32[16,16,8,128]{3,2,1,0:T(8,128)S(1)}, u32[]{:S(2)}, u32[]{:S(2)}) collective-permute-start(f32[16,16,8,128]{3,2,1,0:T(8,128)S(1)} %get-tuple-element.10), channel_id=1, source_target_pairs={{0,1},{1,0},{2,3},{3,2},{4,5},{5,4},{6,7},{7,6},{8,9},{9,8},{10,11... | collective-permute-start | bytes 3145736 | tf_op jit(solution)/shard_map/ppermute | solution.py:137

commit v6 on v5

--- a/solution.py
+++ b/solution.py
@@ -151,7 +151,7 @@
         0,
         axis_index_groups=[[chip_at * 2 + side for chip_at in CHIPS] for side in range(2)],
         tiled=True,
-    ).sum(axis=0)
+    ).sum(axis=0) * scale
     column = lax.all_to_all(
         plane.reshape(n_grp, SUB, width),
         "grp",
@@ -160,7 +160,7 @@
         axis_index_groups=[GROUPS],
         tiled=True,
     )
-    return column.sum(axis=0) * scale
+    return column.sum(axis=0)
 
 
 def solution(mesh):

time: 52.3 us -> 52.4 us (level)
    reduce_sum x1, other arithmetic: 0.02 us -> 0.61 us  [local(): return column.sum(axis=0)]
    mul x1, other arithmetic: 0.6 us -> 0.01 us  [local(): lax.all_to_all(chip.reshape(n_chip, n_grp * SUB, width), 'dev', 0, 0, axi...]
where the time goes in v6:
time: 52.4 us; the launch traced here: 52.1 us
  blocking collectives  42.9 us (82%)
  Pallas kernels  6.29 us (12%)
  starting transfers between devices  1.92 us (4%)
  other arithmetic  0.8 us (2%)
    all_to_all x1, blocking collectives, local(): lax.all_to_all(chip.reshape(n_chip, n_grp * SUB, width), 'dev', 0, 0, axi...  25 us
    all_to_all x1, blocking collectives, local(): lax.all_to_all(plane.reshape(n_grp, SUB, width), 'grp', 0, 0, axis_index_...  17.9 us
    pallas_call x1, Pallas kernels, local(): pl.pallas_call(first_kernel, out_shape=(partial, pltpu.VMEM((rows, 2 * LA...  3.84 us
    pallas_call x1, Pallas kernels, local(): pl.pallas_call(second_kernel, out_shape=partial, in_specs=[vmem, vmem], o...  2.46 us
    ppermute x1, starting transfers between devices, local(): lax.ppermute(theirs, 'dev', [(source, source ^ 1) for source in range(n_d...  1.92 us
  transfers between devices with their start and end apart: 1, of which 1 were waited for; matrix products, arithmetic and copies ran while one was open for 0% of the time, Pallas kernels for 5%

profile of v6, /device:TPU:24, one launch (start us, length us, event | category | flops | bytes accessed | tf_op | source)
XLA Modules:
  0.0 52.1 jit_solution(7069300044761921272)
XLA Ops:
  0.0 3.8 %shard_map.37 = (f32[16,16,8,128]{3,2,1,0:T(8,128)S(1)}, bf16[2048,256]{1,0:T(8,128)(2,1)S(1)}, s32[32,128]{1,0:T(8,128)S(1)}) custom-call(s32[32,128]{1,0:T(8,128)} %bitcast.6, s32[16,128]{1,0:T(8,128)} %bitcast.7, f32[2048,128]{1,0:T(8,128)} %panel_ref.1), custom_call_target="tpu_custom_call" | custom-call | flops 2147483648 | bytes 3145728 | tf_op jit(solution)/shard_map/pallas_call | solution.py:123
  3.8 1.9 %collective-permute-start = (f32[16,16,8,128]{3,2,1,0:T(8,128)S(1)}, f32[16,16,8,128]{3,2,1,0:T(8,128)S(1)}, u32[]{:S(2)}, u32[]{:S(2)}) collective-permute-start(f32[16,16,8,128]{3,2,1,0:T(8,128)S(1)} %get-tuple-element.10), channel_id=1, source_target_pairs={{0,1},{1,0},{2,3},{3,2},{4,5},{5,4},{6,7},{7,6},{8,9},{9,8},{10,11... | collective-permute-start | bytes 3145736 | tf_op jit(solution)/shard_map/ppermute | solution.py:137
  5.8 2.5 %shard_map.38 = f32[16,16,8,128]{3,2,1,0:T(8,128)S(1)} custom-call(s32[32,128]{1,0:T(8,128)S(1)} %get-tuple-element.8.codes_ref, bf16[2048,256]{1,0:T(8,128)(2,1)S(1)} %get-tuple-element.9.split_ref), custom_call_target="tpu_custom_call" | custom-call | flops 2147483648 | bytes 3145728 | tf_op jit(solution)/shard_map/pallas_call | solution.py:138
  8.2 0.2 collective-permute-done
  8.4 0.1 add_bitcast_fusion
  8.5 25.0 %all_to_all.10 = f32[16,128,128]{2,1,0:T(8,128)S(1)} all-to-all(f32[16,128,128]{2,1,0:T(8,128)S(1)} %add_bitcast_fusion), channel_id=1, replica_groups={{20,22,24,26,28,30,0,2,4,6,8,10,12,14,16,18},{21,23,25,27,29,31,1,3,5,7..., dimensions={0} | all-to-all | bytes 2097152 | tf_op jit(solution)/shard_map/all_to_all | solution.py:147
  33.5 0.1 reduce_sum.18
  33.6 17.9 %all_to_all.11 = f32[16,8,128]{2,1,0:T(8,128)S(1)} all-to-all(f32[16,8,128]{2,1,0:T(8,128)S(1)} %multiply_bitcast_fusion), channel_id=1, replica_groups={{288,0,480,32,448,64,416,96,384,128,352,160,320,192,256,224},{289,1,481..., dimensions={0} | all-to-all | bytes 131072 | tf_op jit(solution)/shard_map/all_to_all | solution.py:155
  51.5 0.6 %reduce_sum.19 = f32[8,128]{1,0:T(8,128)} reduce(f32[16,8,128]{2,1,0:T(8,128)S(1)} %all_to_all.11, f32[]{:T(128)} %constant.0.clone.1), dimensions={0}, to_apply=%region_1.0 | reduce | flops 15360 | bytes 69636 | tf_op jit(solution)/shard_map/reduce_sum | solution.py:163
  (1 shorter events, 0.0 us)
Async XLA Ops:
  3.8 4.6 %collective-permute-start = (f32[16,16,8,128]{3,2,1,0:T(8,128)S(1)}, f32[16,16,8,128]{3,2,1,0:T(8,128)S(1)}, u32[]{:S(2)}, u32[]{:S(2)}) collective-permute-start(f32[16,16,8,128]{3,2,1,0:T(8,128)S(1)} %get-tuple-element.10), channel_id=1, source_target_pairs={{0,1},{1,0},{2,3},{3,2},{4,5},{5,4},{6,7},{7,6},{8,9},{9,8},{10,11... | collective-permute-start | bytes 3145736 | tf_op jit(solution)/shard_map/ppermute | solution.py:137
